TPU v7x, 128 devices: a whole 4x4x4 slice. The times are simulated.
128 devices in a mesh: row: 8 (over y_hi, x), col: 16 (over y_lo, z, core).
Axes of the slice: x: 4, y: 4 (y_hi: 2, y_lo: 2; y = y_hi * 2 + y_lo), z: 4, core: 2. Of those that a mesh axis runs over, the one named last changes fastest.
Arguments:
- front_orig: float32 [12288, 12288], P('row', 'col')
- pivot_shift: float32 [12288], replicated, may hold values from 4.5 to 9
- child_update: float32 [16384, 8192], P('row', 'col'), may hold values from -0.046875 to 0.046875
- child_map: int32 [2, 32], replicated, may hold values from 0 to 47, as said below
Outputs:
- front_out: float32 [12288, 12288], P('row', 'col')
Inputs may be any that keep to these rules, and one draw needn't show every extreme that they name: Child h's block b (rows and columns alike) goes to parent block child_map[h, b]; child_map[h, b] % 16 == b % 16; the two child blocks b and b + 16 (b < 16) take two different ones of the parent blocks b, b + 16, b + 32, the smaller child block to the smaller parent block.
All inputs are finite; a program needn't handle non-finite values.
Results may differ from a plain program's by a relative error of at most 0.0001.
Values sent between devices are 32-bit elements; how exact they have to be, the bound alone decides.
No kernel may reach another device: no remote copies, remote signals or barrier semaphores. Data moves between devices by JAX's collectives and lax.ppermute only.
A program may use at most 128 MiB of HBM per device.

v0:
```python
import jax
import jax.numpy as jnp
from jax import lax
from jax.sharding import PartitionSpec as P

BS = 256
PANELS = 6


def from_partner(shard, axis, apart):
    return lax.ppermute(shard, axis, [(i, i ^ 1 << apart) for i in range(lax.axis_size(axis))])


def from_root(shard, axis, root):
    mine = lax.axis_index(axis) == root
    return lax.psum(jnp.where(mine, shard, jnp.zeros_like(shard)), axis)


def symmetric_block(pivot_block):
    return jnp.tril(pivot_block) + jnp.tril(pivot_block, -1).T


def factor_rows(pivot, panel_rows):
    factor = jnp.linalg.cholesky(symmetric_block(pivot))
    below = lax.linalg.triangular_solve(
        factor, panel_rows, left_side=False, lower=True, transpose_a=True
    )
    return (factor, below)


def on_device(front_orig, pivot_shift, child_update, child_map):
    n_row = lax.axis_size("row")
    n_col = lax.axis_size("col")
    row_id = lax.axis_index("row")
    col_id = lax.axis_index("col")
    half_rows = n_row // 2
    local_rows = front_orig.shape[0] // BS
    local_cols = front_orig.shape[1] // BS
    child_rows = child_update.shape[0] // BS
    child_cols = child_update.shape[1] // BS
    pair_count = child_rows // 2
    child_side = row_id // half_rows
    inner_row = row_id % half_rows
    holds_first = child_side == 0
    paired = child_update.reshape(pair_count, 2, BS, child_cols * BS)
    even_blocks = paired[:, 0]
    odd_blocks = paired[:, 1]
    outgoing = jnp.where(holds_first, odd_blocks, even_blocks)
    staying = jnp.where(holds_first, even_blocks, odd_blocks)
    arrived = from_partner(outgoing, "row", half_rows.bit_length() - 1)
    first_part = jnp.where(holds_first, staying, arrived)
    second_part = jnp.where(holds_first, arrived, staying)
    table_index = jnp.arange(child_map.shape[1], dtype=jnp.int32)
    row_wanted = (2 * jnp.arange(pair_count, dtype=jnp.int32) + child_side) * half_rows + inner_row
    col_wanted = jnp.arange(child_cols, dtype=jnp.int32) * n_col + col_id

    def lookup(targets, wanted):
        return jnp.sum(
            jnp.where(wanted[:, None] == table_index[None, :], targets[None, :], 0), axis=1
        )

    def place(part, child_id):
        targets = child_map[child_id]
        row_target = lookup(targets, row_wanted) // n_row
        col_target = lookup(targets, col_wanted) // n_col
        row_pick = (row_target[None, :] == jnp.arange(local_rows, dtype=jnp.int32)[:, None]).astype(
            jnp.float32
        )
        col_pick = (col_target[None, :] == jnp.arange(local_cols, dtype=jnp.int32)[:, None]).astype(
            jnp.float32
        )
        tiles = part.reshape(pair_count, BS, child_cols, BS)
        placed = jnp.einsum(
            "pq,qsjt,kj->pskt", row_pick, tiles, col_pick, precision=lax.Precision.HIGHEST
        )
        return placed.reshape(local_rows * BS, local_cols * BS)

    row_blocks = jnp.arange(local_rows, dtype=jnp.int32) * n_row + row_id
    col_blocks = jnp.arange(local_cols, dtype=jnp.int32) * n_col + col_id
    offsets = jnp.arange(BS, dtype=jnp.int32)
    row_index = (row_blocks[:, None] * BS + offsets[None, :]).reshape(-1)
    col_index = (col_blocks[:, None] * BS + offsets[None, :]).reshape(-1)
    shift_rows = lax.dynamic_index_in_dim(
        pivot_shift.reshape(local_rows, n_row, BS), row_id, axis=1, keepdims=False
    ).reshape(-1)
    diag_term = jnp.where(row_index[:, None] == col_index[None, :], shift_rows[:, None], 0.0)
    front_now = front_orig + diag_term
    front_now = front_now + place(first_part, 0)
    front_now = front_now + place(second_part, 1)
    row_of = jnp.repeat(row_blocks, BS)
    col_of = jnp.repeat(col_blocks, BS)
    stride = n_col // n_row
    pick_index = jnp.arange(local_cols, dtype=jnp.int32) * stride + col_id // n_row
    pick_table = (pick_index[:, None] == jnp.arange(local_rows, dtype=jnp.int32)[None, :]).astype(
        jnp.float32
    )
    level = row_blocks[:, None, None]
    for panel_id in range(PANELS):
        owner_row = panel_id % n_row
        owner_col = panel_id % n_col
        row_slot = panel_id // n_row
        col_slot = panel_id // n_col
        column = front_now[:, col_slot * BS : (col_slot + 1) * BS]
        pivot_local = column[row_slot * BS : (row_slot + 1) * BS]
        pivot = from_root(pivot_local, "row", owner_row)
        factor, own_rows = factor_rows(pivot, column)
        below = from_root(own_rows, "col", owner_col)
        chosen = jnp.einsum(
            "jp,pst->jst",
            pick_table,
            below.reshape(local_rows, BS, BS),
            precision=lax.Precision.HIGHEST,
        )
        across = from_root(chosen.reshape(local_cols * BS, BS), "row", col_id % n_row)
        live = (row_of > panel_id)[:, None] & (col_of > panel_id)[None, :]
        update = jnp.einsum("rk,ck->rc", below, across, precision=lax.Precision.HIGHEST)
        front_now = front_now - jnp.where(live, update, 0.0)
        tiles_now = column.reshape(local_rows, BS, BS)
        below_tiles = below.reshape(local_rows, BS, BS)
        new_column = jnp.where(
            level > panel_id, below_tiles, jnp.where(level == panel_id, factor[None], tiles_now)
        )
        new_column = new_column.reshape(local_rows * BS, BS)
        kept_column = front_now[:, col_slot * BS : (col_slot + 1) * BS]
        front_now = front_now.at[:, col_slot * BS : (col_slot + 1) * BS].set(
            jnp.where(col_id == owner_col, new_column, kept_column)
        )
    return front_now


def solution(mesh):
    in_specs = (P("row", "col"), P(), P("row", "col"), P())
    out_specs = P("row", "col")
    return jax.shard_map(
        on_device, mesh=mesh, in_specs=in_specs, out_specs=out_specs, check_vma=False
    )
```

profile of v0, /device:TPU:0, one launch (start us, length us, event | category | flops | bytes accessed | tf_op | source)
XLA Modules:
  0.0 2403.0 jit_solution(18215019468247353154)
XLA Ops:
  19.4 39.0 %collective-permute-done = f32[4,256,512]{2,1,0:T(8,128)} collective-permute-done((f32[4,256,512]{2,1,0:T(8,128)S(1)}, f32[4,256,512]{2,1,0:T(8,128)}, u32[]{:S(2)}, u32[]{:S(2)}) %collective-permute-start) | collective-permute-done | bytes 2097184 | tf_op jit(solution)/shard_map/ppermute | solution.py:11
  126.6 86.2 %all-reduce.20.cloned.1.call-done = f32[256,256]{0,1:T(8,128)} async-done(((f32[256,256]{0,1:T(8,128)}), f32[256,256]{0,1:T(8,128)}) %all-reduce.20.cloned.1.call-update) | async-done | bytes 262160 | tf_op jit(solution)/shard_map/psum | solution.py:16
  256.5 19.7 custom-call.22
  282.3 119.5 %all-reduce.22.cloned.1.call-done = f32[1536,256]{0,1:T(8,128)} async-done(((f32[1536,256]{0,1:T(8,128)}), f32[1536,256]{0,1:T(8,128)}) %all-reduce.22.cloned.1.call-update) | async-done | bytes 1572880 | tf_op jit(solution)/shard_map/psum | solution.py:16
  409.5 84.5 %all-reduce.24.cloned.1.call-done = f32[768,256]{1,0:T(8,128)} async-done(((f32[768,256]{1,0:T(8,128)}), f32[768,256]{1,0:T(8,128)}) %all-reduce.24.cloned.1.call-update) | async-done | bytes 786448 | tf_op jit(solution)/shard_map/psum | solution.py:16
  507.4 82.4 %all-reduce.26.cloned.1.call-done = f32[256,256]{0,1:T(8,128)} async-done(((f32[256,256]{0,1:T(8,128)}), f32[256,256]{0,1:T(8,128)}) %all-reduce.26.cloned.1.call-update) | async-done | bytes 262160 | tf_op jit(solution)/shard_map/psum | solution.py:16
  632.5 19.7 custom-call.24
  656.0 119.5 %all-reduce.28.cloned.1.call-done = f32[1536,256]{0,1:T(8,128)} async-done(((f32[1536,256]{0,1:T(8,128)}), f32[1536,256]{0,1:T(8,128)}) %all-reduce.28.cloned.1.call-update) | async-done | bytes 1572880 | tf_op jit(solution)/shard_map/psum | solution.py:16
  785.3 82.6 %all-reduce.30.cloned.1.call-done = f32[768,256]{1,0:T(8,128)} async-done(((f32[768,256]{1,0:T(8,128)}), f32[768,256]{1,0:T(8,128)}) %all-reduce.30.cloned.1.call-update) | async-done | bytes 786448 | tf_op jit(solution)/shard_map/psum | solution.py:16
  883.5 82.2 %all-reduce.32.cloned.1.call-done = f32[256,256]{1,0:T(8,128)} async-done(((f32[256,256]{1,0:T(8,128)}), f32[256,256]{1,0:T(8,128)}) %all-reduce.32.cloned.1.call-update) | async-done | bytes 262160 | tf_op jit(solution)/shard_map/psum | solution.py:16
  1008.7 19.7 custom-call.26
  1032.9 119.5 %all-reduce.34.cloned.1.call-done = f32[1536,256]{0,1:T(8,128)} async-done(((f32[1536,256]{0,1:T(8,128)}), f32[1536,256]{0,1:T(8,128)}) %all-reduce.34.cloned.1.call-update) | async-done | bytes 1572880 | tf_op jit(solution)/shard_map/psum | solution.py:16
  1168.1 76.5 %all-reduce.36.cloned.1.call-done = f32[768,256]{1,0:T(8,128)} async-done(((f32[768,256]{1,0:T(8,128)}), f32[768,256]{1,0:T(8,128)}) %all-reduce.36.cloned.1.call-update) | async-done | bytes 786448 | tf_op jit(solution)/shard_map/psum | solution.py:16
  1263.0 82.1 %all-reduce.38.cloned.1.call-done = f32[256,256]{1,0:T(8,128)} async-done(((f32[256,256]{1,0:T(8,128)}), f32[256,256]{1,0:T(8,128)}) %all-reduce.38.cloned.1.call-update) | async-done | bytes 262160 | tf_op jit(solution)/shard_map/psum | solution.py:16
  1388.1 19.7 custom-call.28
  1412.3 119.5 %all-reduce.40.cloned.1.call-done = f32[1536,256]{0,1:T(8,128)} async-done(((f32[1536,256]{0,1:T(8,128)}), f32[1536,256]{0,1:T(8,128)}) %all-reduce.40.cloned.1.call-update) | async-done | bytes 1572880 | tf_op jit(solution)/shard_map/psum | solution.py:16
  1537.1 87.0 %all-reduce.42.cloned.1.call-done = f32[768,256]{1,0:T(8,128)} async-done(((f32[768,256]{1,0:T(8,128)}), f32[768,256]{1,0:T(8,128)}) %all-reduce.42.cloned.1.call-update) | async-done | bytes 786448 | tf_op jit(solution)/shard_map/psum | solution.py:16
  1642.1 82.2 %all-reduce.44.cloned.1.call-done = f32[256,256]{1,0:T(8,128)} async-done(((f32[256,256]{1,0:T(8,128)}), f32[256,256]{1,0:T(8,128)}) %all-reduce.44.cloned.1.call-update) | async-done | bytes 262160 | tf_op jit(solution)/shard_map/psum | solution.py:16
  1791.4 119.5 %all-reduce.46.cloned.1.call-done = f32[1536,256]{0,1:T(8,128)} async-done(((f32[1536,256]{0,1:T(8,128)}), f32[1536,256]{0,1:T(8,128)}) %all-reduce.46.cloned.1.call-update) | async-done | bytes 1572880 | tf_op jit(solution)/shard_map/psum | solution.py:16
  1916.2 87.0 %all-reduce.48.cloned.1.call-done = f32[768,256]{1,0:T(8,128)} async-done(((f32[768,256]{1,0:T(8,128)}), f32[768,256]{1,0:T(8,128)}) %all-reduce.48.cloned.1.call-update) | async-done | bytes 786448 | tf_op jit(solution)/shard_map/psum | solution.py:16
  2017.6 82.1 %all-reduce.50.cloned.1.call-done = f32[256,256]{1,0:T(8,128)} async-done(((f32[256,256]{1,0:T(8,128)}), f32[256,256]{1,0:T(8,128)}) %all-reduce.50.cloned.1.call-update) | async-done | bytes 262160 | tf_op jit(solution)/shard_map/psum | solution.py:16
  2142.9 19.7 custom-call.32
  2167.1 119.5 %all-reduce.52.cloned.1.call-done = f32[1536,256]{0,1:T(8,128)} async-done(((f32[1536,256]{0,1:T(8,128)}), f32[1536,256]{0,1:T(8,128)}) %all-reduce.52.cloned.1.call-update) | async-done | bytes 1572880 | tf_op jit(solution)/shard_map/psum | solution.py:16
  2293.8 85.0 %all-reduce.54.cloned.1.call-done = f32[768,256]{1,0:T(8,128)} async-done(((f32[768,256]{1,0:T(8,128)}), f32[768,256]{1,0:T(8,128)}) %all-reduce.54.cloned.1.call-update) | async-done | bytes 786448 | tf_op jit(solution)/shard_map/psum | solution.py:16
  (390 shorter events, 549.7 us)
Async XLA Ops:
  6.5 206.3 %all-reduce.20.cloned.1.call-start = ((), (), s32[]{:S(2)}) async-start(), calls=%async_computation | async-start | bytes 524288 | tf_op jit(solution)/shard_map/psum | solution.py:16
  9.2 49.1 %collective-permute-start = (f32[4,256,512]{2,1,0:T(8,128)S(1)}, f32[4,256,512]{2,1,0:T(8,128)}, u32[]{:S(2)}, u32[]{:S(2)}) collective-permute-start(f32[4,256,512]{2,1,0:T(8,128)S(1)} %select_bitcast_fusion), channel_id=1, source_target_pairs={{0,64},{16,80},{32,96},{48,112},{64,0},{80,16},{96,32},{112,48},{1... | collective-permute-start | bytes 6291464 | tf_op jit(solution)/shard_map/ppermute | solution.py:11
  125.9 275.9 %all-reduce.22.cloned.1.call-start = ((), (), s32[]{:S(2)}) async-start(), calls=%async_computation.1 | async-start | bytes 3145728 | tf_op jit(solution)/shard_map/psum | solution.py:16
  282.2 211.8 %all-reduce.24.cloned.1.call-start = ((), (), s32[]{:S(2)}) async-start(), calls=%async_computation.2 | async-start | bytes 1572864 | tf_op jit(solution)/shard_map/psum | solution.py:16
  406.7 183.1 %all-reduce.26.cloned.1.call-start = ((), (), s32[]{:S(2)}) async-start(), calls=%async_computation.3 | async-start | bytes 524288 | tf_op jit(solution)/shard_map/psum | solution.py:16
  407.9 86.2 %copy-start.9 = (f32[1536,256]{0,1:T(8,128)S(1)}, f32[1536,256]{0,1:T(8,128)}, u32[]{:S(2)}) copy-start(f32[1536,256]{0,1:T(8,128)} %all-reduce.22.cloned.1.call-done) | copy-start | bytes 4718596
  507.1 268.4 %all-reduce.28.cloned.1.call-start = ((), (), s32[]{:S(2)}) async-start(), calls=%async_computation.4 | async-start | bytes 3145728 | tf_op jit(solution)/shard_map/psum | solution.py:16
  656.0 211.9 %all-reduce.30.cloned.1.call-start = ((), (), s32[]{:S(2)}) async-start(), calls=%async_computation.5 | async-start | bytes 1572864 | tf_op jit(solution)/shard_map/psum | solution.py:16
  780.5 185.1 %all-reduce.32.cloned.1.call-start = ((), (), s32[]{:S(2)}) async-start(), calls=%async_computation.6 | async-start | bytes 524288 | tf_op jit(solution)/shard_map/psum | solution.py:16
  782.2 85.8 %copy-start.10 = (f32[1536,256]{0,1:T(8,128)S(1)}, f32[1536,256]{0,1:T(8,128)}, u32[]{:S(2)}) copy-start(f32[1536,256]{0,1:T(8,128)} %all-reduce.28.cloned.1.call-done) | copy-start | bytes 4718596
  883.0 269.4 %all-reduce.34.cloned.1.call-start = ((), (), s32[]{:S(2)}) async-start(), calls=%async_computation.7 | async-start | bytes 3145728 | tf_op jit(solution)/shard_map/psum | solution.py:16
  1032.8 211.8 %all-reduce.36.cloned.1.call-start = ((), (), s32[]{:S(2)}) async-start(), calls=%async_computation.8 | async-start | bytes 1572864 | tf_op jit(solution)/shard_map/psum | solution.py:16
  1157.3 187.9 %all-reduce.38.cloned.1.call-start = ((), (), s32[]{:S(2)}) async-start(), calls=%async_computation.9 | async-start | bytes 524288 | tf_op jit(solution)/shard_map/psum | solution.py:16
  1262.6 269.3 %all-reduce.40.cloned.1.call-start = ((), (), s32[]{:S(2)}) async-start(), calls=%async_computation.10 | async-start | bytes 3145728 | tf_op jit(solution)/shard_map/psum | solution.py:16
  1412.3 211.9 %all-reduce.42.cloned.1.call-start = ((), (), s32[]{:S(2)}) async-start(), calls=%async_computation.11 | async-start | bytes 1572864 | tf_op jit(solution)/shard_map/psum | solution.py:16
  1535.7 88.4 %copy-start.12 = (f32[1536,256]{0,1:T(8,128)S(1)}, f32[1536,256]{0,1:T(8,128)}, u32[]{:S(2)}) copy-start(f32[1536,256]{0,1:T(8,128)} %all-reduce.40.cloned.1.call-done) | copy-start | bytes 4718596
  1536.7 187.5 %all-reduce.44.cloned.1.call-start = ((), (), s32[]{:S(2)}) async-start(), calls=%async_computation.12 | async-start | bytes 524288 | tf_op jit(solution)/shard_map/psum | solution.py:16
  1640.9 146.9 %copy-start.4 = (f32[1536,256]{1,0:T(8,128)}, f32[1536,256]{1,0:T(8,128)S(1)}, u32[]{:S(2)}) copy-start(f32[1536,256]{1,0:T(8,128)S(1)} %get-tuple-element.244) | copy-start | bytes 4718596
  1641.6 269.3 %all-reduce.46.cloned.1.call-start = ((), (), s32[]{:S(2)}) async-start(), calls=%async_computation.13 | async-start | bytes 3145728 | tf_op jit(solution)/shard_map/psum | solution.py:16
  1791.4 211.8 %all-reduce.48.cloned.1.call-start = ((), (), s32[]{:S(2)}) async-start(), calls=%async_computation.14 | async-start | bytes 1572864 | tf_op jit(solution)/shard_map/psum | solution.py:16
  1914.8 88.4 %copy-start.13 = (f32[1536,256]{0,1:T(8,128)S(1)}, f32[1536,256]{0,1:T(8,128)}, u32[]{:S(2)}) copy-start(f32[1536,256]{0,1:T(8,128)} %all-reduce.46.cloned.1.call-done) | copy-start | bytes 4718596
  1915.8 183.9 %all-reduce.50.cloned.1.call-start = ((), (), s32[]{:S(2)}) async-start(), calls=%async_computation.15 | async-start | bytes 524288 | tf_op jit(solution)/shard_map/psum | solution.py:16
  2017.2 269.4 %all-reduce.52.cloned.1.call-start = ((), (), s32[]{:S(2)}) async-start(), calls=%async_computation.16 | async-start | bytes 3145728 | tf_op jit(solution)/shard_map/psum | solution.py:16
  2167.0 211.8 %all-reduce.54.cloned.1.call-start = ((), (), s32[]{:S(2)}) async-start(), calls=%async_computation.17 | async-start | bytes 1572864 | tf_op jit(solution)/shard_map/psum | solution.py:16
  (17 other events, 155.1 us)
Sparse Core Ops, SparseCore 0:
  126.0 86.8 all-reduce.19
  282.4 119.3 all-reduce.21
  406.8 87.1 all-reduce.23
  507.3 82.4 all-reduce.25
  656.1 119.3 all-reduce.27
  780.7 87.2 all-reduce.29
  883.1 82.4 all-reduce.31
  1032.9 119.3 all-reduce.33
  1157.4 87.1 all-reduce.35
  1262.7 82.4 all-reduce.37
  1412.4 119.4 all-reduce.39
  1536.9 87.2 all-reduce.41
  1641.8 82.4 all-reduce.43
  1791.5 119.3 all-reduce.45
  1916.0 87.1 all-reduce.47
  2017.3 82.4 all-reduce.49
  2167.1 119.3 all-reduce.51
  2291.6 87.2 all-reduce.53
where the time goes:
time: 2410 us; the launch traced here: 2400 us
  waiting for transfers between devices  1760 us (73%)
  other arithmetic  380 us (16%)
  matrix products  120 us (5%)
  local copies, waits for them, and re-layouts  117 us (5%)
    psum x18, waiting for transfers between devices, from_root(): return lax.psum(jnp.where(mine, shard, jnp.zeros_like(shard)), axis)  1720 us
    another operation x42, other arithmetic, factor_rows(): factor = jnp.linalg.cholesky(symmetric_block(pivot))  208 us
    another operation x13, other arithmetic, factor_rows(): lax.linalg.triangular_solve(factor, panel_rows, left_side=False, lower=Tr...  118 us
    dot_general x6, matrix products, on_device(): jnp.einsum('rk,ck->rc', below, across, precision=lax.Precision.HIGHEST)  63.6 us
  transfers between devices with their start and end apart: 19, of which 19 were waited for; matrix products, arithmetic and copies ran while one was open for 1% of the time, Pallas kernels for 0%

commit v1 on v0

--- a/solution.py
+++ b/solution.py
@@ -13,7 +13,7 @@
 
 def from_root(shard, axis, root):
     mine = lax.axis_index(axis) == root
-    return lax.psum(jnp.where(mine, shard, jnp.zeros_like(shard)), axis)
+    return jnp.sum(lax.all_gather(jnp.where(mine, shard, jnp.zeros_like(shard)), axis), axis=0)
 
 
 def symmetric_block(pivot_block):

time: 2410 us -> 2550 us (1.058)
  local copies, waits for them, and re-layouts: 117 us -> 285 us
  waiting for transfers between devices: 1760 us -> 1680 us
  other arithmetic: 380 us -> 440 us
    psum x18 -> x0, waiting for transfers between devices: 1720 us -> none  [from_root(): return lax.psum(jnp.where(mine, shard, jnp.zeros_like(shard)), axis)]
    all_gather x0 -> x18, waiting for transfers between devices: none -> 1640 us  [from_root(): lax.all_gather(jnp.where(mine, shard, jnp.zeros_like(shard)), axis)]
    unnamed x47 -> x55, local copies, waits for them, and re-layouts: 24.9 us -> 195 us
    reduce_sum x0 -> x18, other arithmetic: none -> 64.3 us  [from_root(): jnp.sum(lax.all_gather(jnp.where(mine, shard, jnp.zeros_like(shard)), axi...]
where the time goes in v1:
time: 2550 us; the launch traced here: 2540 us
  waiting for transfers between devices  1680 us (66%)
  other arithmetic  440 us (17%)
  local copies, waits for them, and re-layouts  285 us (11%)
  matrix products  107 us (4%)
    all_gather x18, waiting for transfers between devices, from_root(): lax.all_gather(jnp.where(mine, shard, jnp.zeros_like(shard)), axis)  1640 us
    another operation x42, other arithmetic, factor_rows(): factor = jnp.linalg.cholesky(symmetric_block(pivot))  208 us
    unnamed x55, local copies, waits for them, and re-layouts  195 us
    another operation x13, other arithmetic, factor_rows(): lax.linalg.triangular_solve(factor, panel_rows, left_side=False, lower=Tr...  118 us
    reduce_sum x18, other arithmetic, from_root(): jnp.sum(lax.all_gather(jnp.where(mine, shard, jnp.zeros_like(shard)), axi...  64.3 us
  transfers between devices with their start and end apart: 19, of which 19 were waited for; matrix products, arithmetic and copies ran while one was open for 1% of the time, Pallas kernels for 0%

profile of v1, /device:TPU:0, one launch (start us, length us, event | category | flops | bytes accessed | tf_op | source)
XLA Modules:
  0.0 2537.6 jit_solution(7345890649236793686)
XLA Ops:
  19.3 39.0 %collective-permute-done = f32[4,256,512]{2,1,0:T(8,128)} collective-permute-done((f32[4,256,512]{2,1,0:T(8,128)S(1)}, f32[4,256,512]{2,1,0:T(8,128)}, u32[]{:S(2)}, u32[]{:S(2)}) %collective-permute-start) | collective-permute-done | bytes 2097184 | tf_op jit(solution)/shard_map/ppermute | solution.py:11
  126.4 59.5 %all-gather.43.cloned.1.call-done = f32[2048,256]{0,1:T(8,128)} async-done(((f32[256,256]{0,1:T(8,128)}), f32[2048,256]{0,1:T(8,128)}) %all-gather.43.cloned.1.call-update) | async-done | bytes 2097168 | tf_op jit(solution)/shard_map/all_gather | solution.py:16
  256.1 130.1 %all-gather.45.cloned.1.call-done = f32[24576,256]{0,1:T(8,128)} async-done(((f32[1536,256]{0,1:T(8,128)}), f32[24576,256]{0,1:T(8,128)}) %all-gather.45.cloned.1.call-update) | async-done | bytes 25165840 | tf_op jit(solution)/shard_map/all_gather | solution.py:16
  386.2 26.0 %copy.351 = f32[32,8,16,1536]{3,2,1,0:T(8,128)S(1)} copy(f32[32,8,16,1536]{3,1,2,0:T(8,128)} %bitcast.368) | data formatting | bytes 50331648
  424.8 87.9 %all-gather.31.cloned.1.call-done = f32[8,768,256]{2,1,0:T(8,128)} async-done(((f32[1,768,256]{2,1,0:T(8,128)}), f32[8,768,256]{2,1,0:T(8,128)}) %all-gather.31.cloned.1.call-update) | async-done | bytes 6291472 | tf_op jit(solution)/shard_map/all_gather | solution.py:16
  529.5 55.1 %all-gather.47.cloned.1.call-done = f32[2048,256]{0,1:T(8,128)} async-done(((f32[256,256]{0,1:T(8,128)}), f32[2048,256]{0,1:T(8,128)}) %all-gather.47.cloned.1.call-update) | async-done | bytes 2097168 | tf_op jit(solution)/shard_map/all_gather | solution.py:16
  652.5 130.1 %all-gather.49.cloned.1.call-done = f32[24576,256]{0,1:T(8,128)} async-done(((f32[1536,256]{0,1:T(8,128)}), f32[24576,256]{0,1:T(8,128)}) %all-gather.49.cloned.1.call-update) | async-done | bytes 25165840 | tf_op jit(solution)/shard_map/all_gather | solution.py:16
  782.6 26.0 %copy.353 = f32[32,8,16,1536]{3,2,1,0:T(8,128)S(1)} copy(f32[32,8,16,1536]{3,1,2,0:T(8,128)} %bitcast.369) | data formatting | bytes 50331648
  820.5 88.6 %all-gather.33.cloned.1.call-done = f32[8,768,256]{2,1,0:T(8,128)} async-done(((f32[1,768,256]{2,1,0:T(8,128)}), f32[8,768,256]{2,1,0:T(8,128)}) %all-gather.33.cloned.1.call-update) | async-done | bytes 6291472 | tf_op jit(solution)/shard_map/all_gather | solution.py:16
  925.3 55.1 %all-gather.51.cloned.1.call-done = f32[2048,256]{0,1:T(8,128)} async-done(((f32[256,256]{0,1:T(8,128)}), f32[2048,256]{0,1:T(8,128)}) %all-gather.51.cloned.1.call-update) | async-done | bytes 2097168 | tf_op jit(solution)/shard_map/all_gather | solution.py:16
  1048.2 130.1 %all-gather.53.cloned.1.call-done = f32[24576,256]{0,1:T(8,128)} async-done(((f32[1536,256]{0,1:T(8,128)}), f32[24576,256]{0,1:T(8,128)}) %all-gather.53.cloned.1.call-update) | async-done | bytes 25165840 | tf_op jit(solution)/shard_map/all_gather | solution.py:16
  1178.3 26.0 %copy.355 = f32[32,8,16,1536]{3,2,1,0:T(8,128)S(1)} copy(f32[32,8,16,1536]{3,1,2,0:T(8,128)} %bitcast.370) | data formatting | bytes 50331648
  1221.3 86.0 %all-gather.35.cloned.1.call-done = f32[8,768,256]{2,1,0:T(8,128)} async-done(((f32[1,768,256]{2,1,0:T(8,128)}), f32[8,768,256]{2,1,0:T(8,128)}) %all-gather.35.cloned.1.call-update) | async-done | bytes 6291472 | tf_op jit(solution)/shard_map/all_gather | solution.py:16
  1325.7 55.1 %all-gather.55.cloned.1.call-done = f32[2048,256]{0,1:T(8,128)} async-done(((f32[256,256]{0,1:T(8,128)}), f32[2048,256]{0,1:T(8,128)}) %all-gather.55.cloned.1.call-update) | async-done | bytes 2097168 | tf_op jit(solution)/shard_map/all_gather | solution.py:16
  1448.5 130.1 %all-gather.57.cloned.1.call-done = f32[24576,256]{0,1:T(8,128)} async-done(((f32[1536,256]{0,1:T(8,128)}), f32[24576,256]{0,1:T(8,128)}) %all-gather.57.cloned.1.call-update) | async-done | bytes 25165840 | tf_op jit(solution)/shard_map/all_gather | solution.py:16
  1578.6 26.0 %copy.357 = f32[32,8,16,1536]{3,2,1,0:T(8,128)S(1)} copy(f32[32,8,16,1536]{3,1,2,0:T(8,128)} %bitcast.371) | data formatting | bytes 50331648
  1621.6 86.0 %all-gather.37.cloned.1.call-done = f32[8,768,256]{2,1,0:T(8,128)} async-done(((f32[1,768,256]{2,1,0:T(8,128)}), f32[8,768,256]{2,1,0:T(8,128)}) %all-gather.37.cloned.1.call-update) | async-done | bytes 6291472 | tf_op jit(solution)/shard_map/all_gather | solution.py:16
  1726.0 55.1 %all-gather.59.cloned.1.call-done = f32[2048,256]{0,1:T(8,128)} async-done(((f32[256,256]{0,1:T(8,128)}), f32[2048,256]{0,1:T(8,128)}) %all-gather.59.cloned.1.call-update) | async-done | bytes 2097168 | tf_op jit(solution)/shard_map/all_gather | solution.py:16
  1848.8 130.1 %all-gather.61.cloned.1.call-done = f32[24576,256]{0,1:T(8,128)} async-done(((f32[1536,256]{0,1:T(8,128)}), f32[24576,256]{0,1:T(8,128)}) %all-gather.61.cloned.1.call-update) | async-done | bytes 25165840 | tf_op jit(solution)/shard_map/all_gather | solution.py:16
  1978.9 26.0 %copy.359 = f32[32,8,16,1536]{3,2,1,0:T(8,128)S(1)} copy(f32[32,8,16,1536]{3,1,2,0:T(8,128)} %bitcast.372) | data formatting | bytes 50331648
  2021.9 86.0 %all-gather.39.cloned.1.call-done = f32[8,768,256]{2,1,0:T(8,128)} async-done(((f32[1,768,256]{2,1,0:T(8,128)}), f32[8,768,256]{2,1,0:T(8,128)}) %all-gather.39.cloned.1.call-update) | async-done | bytes 6291472 | tf_op jit(solution)/shard_map/all_gather | solution.py:16
  2126.3 55.1 %all-gather.63.cloned.1.call-done = f32[2048,256]{0,1:T(8,128)} async-done(((f32[256,256]{0,1:T(8,128)}), f32[2048,256]{0,1:T(8,128)}) %all-gather.63.cloned.1.call-update) | async-done | bytes 2097168 | tf_op jit(solution)/shard_map/all_gather | solution.py:16
  2249.2 130.1 %all-gather.65.cloned.1.call-done = f32[24576,256]{0,1:T(8,128)} async-done(((f32[1536,256]{0,1:T(8,128)}), f32[24576,256]{0,1:T(8,128)}) %all-gather.65.cloned.1.call-update) | async-done | bytes 25165840 | tf_op jit(solution)/shard_map/all_gather | solution.py:16
  2422.3 86.1 %all-gather.41.cloned.1.call-done = f32[8,768,256]{2,1,0:T(8,128)} async-done(((f32[1,768,256]{2,1,0:T(8,128)}), f32[8,768,256]{2,1,0:T(8,128)}) %all-gather.41.cloned.1.call-update) | async-done | bytes 6291472 | tf_op jit(solution)/shard_map/all_gather | solution.py:16
  (411 shorter events, 733.7 us)
Async XLA Ops:
  6.5 179.4 %all-gather.43.cloned.1.call-start = ((), (), s32[]{:S(2)}) async-start(), calls=%async_computation.6 | async-start | bytes 2359296 | tf_op jit(solution)/shard_map/all_gather | solution.py:16
  9.2 49.1 %collective-permute-start = (f32[4,256,512]{2,1,0:T(8,128)S(1)}, f32[4,256,512]{2,1,0:T(8,128)}, u32[]{:S(2)}, u32[]{:S(2)}) collective-permute-start(f32[4,256,512]{2,1,0:T(8,128)S(1)} %select_bitcast_fusion), channel_id=1, source_target_pairs={{0,64},{16,80},{32,96},{48,112},{64,0},{80,16},{96,32},{112,48},{1... | collective-permute-start | bytes 6291464 | tf_op jit(solution)/shard_map/ppermute | solution.py:11
  125.9 260.3 %all-gather.45.cloned.1.call-start = ((), (), s32[]{:S(2)}) async-start(), calls=%async_computation.7 | async-start | bytes 26738688 | tf_op jit(solution)/shard_map/all_gather | solution.py:16
  256.0 256.7 %all-gather.31.cloned.1.call-start = ((), (), s32[]{:S(2)}) async-start(), calls=%async_computation | async-start | bytes 7077888 | tf_op jit(solution)/shard_map/all_gather | solution.py:16
  422.0 162.6 %all-gather.47.cloned.1.call-start = ((), (), s32[]{:S(2)}) async-start(), calls=%async_computation.8 | async-start | bytes 2359296 | tf_op jit(solution)/shard_map/all_gather | solution.py:16
  528.3 121.2 %copy-start.5 = (f32[1536,256]{0,1:T(8,128)}, f32[1536,256]{0,1:T(8,128)S(1)}, u32[]{:S(2)}) copy-start(f32[1536,256]{0,1:T(8,128)S(1)} %get-tuple-element.194) | copy-start | bytes 4718596
  529.1 253.5 %all-gather.49.cloned.1.call-start = ((), (), s32[]{:S(2)}) async-start(), calls=%async_computation.9 | async-start | bytes 26738688 | tf_op jit(solution)/shard_map/all_gather | solution.py:16
  652.4 256.6 %all-gather.33.cloned.1.call-start = ((), (), s32[]{:S(2)}) async-start(), calls=%async_computation.1 | async-start | bytes 7077888 | tf_op jit(solution)/shard_map/all_gather | solution.py:16
  818.4 162.0 %all-gather.51.cloned.1.call-start = ((), (), s32[]{:S(2)}) async-start(), calls=%async_computation.10 | async-start | bytes 2359296 | tf_op jit(solution)/shard_map/all_gather | solution.py:16
  924.8 253.5 %all-gather.53.cloned.1.call-start = ((), (), s32[]{:S(2)}) async-start(), calls=%async_computation.11 | async-start | bytes 26738688 | tf_op jit(solution)/shard_map/all_gather | solution.py:16
  1048.2 259.2 %all-gather.35.cloned.1.call-start = ((), (), s32[]{:S(2)}) async-start(), calls=%async_computation.2 | async-start | bytes 7077888 | tf_op jit(solution)/shard_map/all_gather | solution.py:16
  1216.6 164.2 %all-gather.55.cloned.1.call-start = ((), (), s32[]{:S(2)}) async-start(), calls=%async_computation.12 | async-start | bytes 2359296 | tf_op jit(solution)/shard_map/all_gather | solution.py:16
  1325.3 253.3 %all-gather.57.cloned.1.call-start = ((), (), s32[]{:S(2)}) async-start(), calls=%async_computation.13 | async-start | bytes 26738688 | tf_op jit(solution)/shard_map/all_gather | solution.py:16
  1384.2 60.3 %copy-start.2 = (f32[1536,256]{0,1:T(8,128)S(1)}, f32[1536,256]{0,1:T(8,128)}, u32[]{:S(2)}) copy-start(f32[1536,256]{0,1:T(8,128)} %copy-done.1) | copy-start | bytes 4718596
  1448.5 259.2 %all-gather.37.cloned.1.call-start = ((), (), s32[]{:S(2)}) async-start(), calls=%async_computation.3 | async-start | bytes 7077888 | tf_op jit(solution)/shard_map/all_gather | solution.py:16
  1616.9 164.2 %all-gather.59.cloned.1.call-start = ((), (), s32[]{:S(2)}) async-start(), calls=%async_computation.14 | async-start | bytes 2359296 | tf_op jit(solution)/shard_map/all_gather | solution.py:16
  1725.6 253.3 %all-gather.61.cloned.1.call-start = ((), (), s32[]{:S(2)}) async-start(), calls=%async_computation.15 | async-start | bytes 26738688 | tf_op jit(solution)/shard_map/all_gather | solution.py:16
  1784.5 60.3 %copy-start.4 = (f32[1536,256]{0,1:T(8,128)S(1)}, f32[1536,256]{0,1:T(8,128)}, u32[]{:S(2)}) copy-start(f32[1536,256]{0,1:T(8,128)} %copy-done.3) | copy-start | bytes 4718596
  1848.8 259.2 %all-gather.39.cloned.1.call-start = ((), (), s32[]{:S(2)}) async-start(), calls=%async_computation.4 | async-start | bytes 7077888 | tf_op jit(solution)/shard_map/all_gather | solution.py:16
  2017.2 164.2 %all-gather.63.cloned.1.call-start = ((), (), s32[]{:S(2)}) async-start(), calls=%async_computation.16 | async-start | bytes 2359296 | tf_op jit(solution)/shard_map/all_gather | solution.py:16
  2125.9 253.5 %all-gather.65.cloned.1.call-start = ((), (), s32[]{:S(2)}) async-start(), calls=%async_computation.17 | async-start | bytes 26738688 | tf_op jit(solution)/shard_map/all_gather | solution.py:16
  2184.8 60.4 %copy-start.8 = (f32[1536,256]{0,1:T(8,128)S(1)}, f32[1536,256]{0,1:T(8,128)}, u32[]{:S(2)}) copy-start(f32[1536,256]{0,1:T(8,128)} %copy-done.7) | copy-start | bytes 4718596
  2249.2 259.2 %all-gather.41.cloned.1.call-start = ((), (), s32[]{:S(2)}) async-start(), calls=%async_computation.5 | async-start | bytes 7077888 | tf_op jit(solution)/shard_map/all_gather | solution.py:16
  2512.6 8.0 copy-start.15
  (15 other events, 83.4 us)
Sparse Core Ops, SparseCore 0:
  126.0 59.8 all-gather.42
  256.1 129.9 all-gather.44
  422.1 90.5 all-gather.30
  529.2 55.3 all-gather.46
  652.6 129.9 all-gather.48
  818.5 90.5 all-gather.32
  925.0 55.3 all-gather.50
  1048.3 129.9 all-gather.52
  1216.7 90.5 all-gather.34
  1325.4 55.3 all-gather.54
  1448.6 129.9 all-gather.56
  1617.0 90.5 all-gather.36
  1725.7 55.3 all-gather.58
  1848.9 129.9 all-gather.60
  2017.3 90.5 all-gather.38
  2126.0 55.3 all-gather.62
  2249.3 129.9 all-gather.64
  2417.8 90.5 all-gather.40
